TPU v7x, 32 devices: a whole 2x2x4 slice. The times are simulated.
32 devices in a mesh: groups: 2 (over x), outer: 4 (over z), inner: 4 (over y, core).
Axes of the slice: x: 2, y: 2, z: 4, core: 2. Of those that a mesh axis runs over, the one named last changes fastest.
Arguments:
- grid_feats: bfloat16 [16384, 1024], P(('groups', 'outer', 'inner')), parts along dimension 0, may hold values from -610 to 610
- mesh_feats: bfloat16 [8192, 1024], P(('groups', 'outer', 'inner')), parts along dimension 0, may hold values from -610 to 610
- routes: int32 [512, 4], P(('groups', 'outer', 'inner')), parts along dimension 0, may hold values from 0 to 15, all different within a row; in each aligned block of 16 rows (0 to 15, 16 to 31, ...) at most 4 rows name the same one
- edge_first: int32 [8192, 4], P(('groups', 'outer', 'inner')), parts along dimension 0, may hold values from 0 to 511, as said below
- edge_count: int32 [8192, 4], P(('groups', 'outer', 'inner')), parts along dimension 0, may hold values from 1 to 256
- w_query: bfloat16 [1024, 512], replicated, may hold values from -6 to 6
- w_kv: bfloat16 [1024, 1024], replicated, may hold values from -0.1875 to 0.1875
- w_out_enc: bfloat16 [512, 1024], replicated, may hold values from -2 to 2
- w_qkv: bfloat16 [1024, 1536], replicated, may hold values from -6 to 6
- w_out_proc: bfloat16 [512, 1024], replicated, may hold values from -2 to 2
Outputs:
- encoded: bfloat16 [8192, 1024], P(('groups', 'outer', 'inner')), parts along dimension 0
- processed: bfloat16 [8192, 1024], P(('groups', 'outer', 'inner')), parts along dimension 0
There are 2 independent parts, one for each index of `groups`. A program takes and returns all parts, laid end to end along the dimension named above; an argument that names none is the same for every part. Nothing has to cross between parts.
Inputs may be any that keep to these rules, and one draw needn't show every extreme that they name: `routes`: in the rows of one device (16 blocks) no owner is named more than 4 times, a bound that some block reaches; each row names 4 different owners. edge_first + edge_count <= 512.
All inputs are finite; a program needn't handle non-finite values.
Results may differ from a plain program's by a relative error of at most 0.039.
Values may be sent and summed in bfloat16 or wider, within the bound.
No kernel may reach another device: no remote copies, remote signals or barrier semaphores. Data moves between devices by JAX's collectives and lax.ppermute only.
A program may use at most 64 MiB of HBM per device.

v0:
```python
import functools
import math

import jax
import jax.numpy as jnp
from jax import lax
from jax.experimental import pallas as pl
from jax.experimental.pallas import tpu as pltpu
from jax.sharding import PartitionSpec as P


HEADS = 8
LANES = 128
NEG = -1e30
AXES = ("outer", "inner")
VMEM = pl.BlockSpec(memory_space=pltpu.VMEM)
SMEM = pl.BlockSpec(memory_space=pltpu.SMEM)
ANY = pl.BlockSpec(memory_space=pl.ANY)
HBM = pl.BlockSpec(memory_space=pltpu.HBM)
LIMIT = 50 << 20


def norm_rows(inputs):
    as_float = inputs.astype(jnp.float32)
    row_mean = jnp.mean(as_float, axis=-1, keepdims=True)
    centered = as_float - row_mean
    variance = jnp.mean(centered * centered, axis=-1, keepdims=True)
    return (centered * lax.rsqrt(variance + 1e-05)).astype(jnp.bfloat16)


def mm(a, b):
    return jnp.dot(a, b, preferred_element_type=jnp.float32)


def mm_nt(a, b):
    return lax.dot_general(a, b, (((1,), (1,)), ((), ())), preferred_element_type=jnp.float32)


def mm_tn(a, b):
    return lax.dot_general(a, b, (((0,), (0,)), ((), ())), preferred_element_type=jnp.float32)


def lane_group(shape, width):
    return lax.broadcasted_iota(jnp.int32, shape, len(shape) - 1) // width


def half_masks():
    low = (lane_group((1, LANES), LANES // 2) == 0).astype(jnp.float32)
    return low.astype(jnp.bfloat16), (1.0 - low).astype(jnp.bfloat16)


def fetch(pairs, sems):
    copies = [pltpu.make_async_copy(src, dst, sems.at[i]) for i, (src, dst) in enumerate(pairs)]
    for item in copies:
        item.start()
    return copies


def send_kernel(block_len, capacity, query_scale, routes_h, first_h, count_h, mesh_h, w_query_h, send, ranks,
                routes, first, count, mesh, w_query, tally, notes, sems):
    copies = fetch(
        [(mesh_h, mesh), (w_query_h, w_query), (routes_h, routes), (first_h, first), (count_h, count)], sems
    )
    route_count, block_count = routes.shape
    node_count = send.shape[0]
    pair_rows = capacity * block_len
    pairs = w_query.shape[1] // LANES
    note_rows = send.shape[1] - pairs * pair_rows

    def clear(i, carry):
        tally[i] = 0
        return carry

    lax.fori_loop(0, node_count, clear, 0)
    if node_count * capacity != block_count * route_count:
        send[...] = jnp.zeros(send.shape, send.dtype)
    notes[...] = jnp.zeros(notes.shape, notes.dtype)
    copies[0].wait()
    normed = norm_rows(mesh[...])
    for item in copies[1:]:
        item.wait()
    first_all = first[...]
    upper = first_all >= 256
    low_part = jnp.where(upper, first_all - 256, first_all).astype(jnp.float32)
    signed = jnp.where(upper, -count[...], count[...]).astype(jnp.float32)
    group = lane_group((1, LANES), block_len)
    per_tile = LANES // block_len
    queries = (mm(normed, w_query[...]) * query_scale).astype(jnp.bfloat16)
    for block in range(block_count):
        tile, spot = divmod(block, per_tile)
        cols = slice(tile * LANES, (tile + 1) * LANES)
        rows = slice(block * block_len, (block + 1) * block_len)
        for route in range(route_count):
            owner = routes[route, block]
            rank = tally[owner]
            tally[owner] = rank + 1
            ranks[route, block] = rank
            for pair in range(pairs):
                start = pl.multiple_of(pair * pair_rows + rank * block_len, block_len)
                send[owner, pl.ds(start, block_len), :] = queries[rows, pair * LANES:(pair + 1) * LANES]
            note = owner * note_rows + 2 * rank
            keep = group == spot
            notes[pl.ds(note, 1), :] = jnp.where(keep, low_part[route:route + 1, cols], 0.0)
            notes[pl.ds(note + 1, 1), :] = jnp.where(keep, signed[route:route + 1, cols], 0.0)
    for owner in range(node_count):
        send[owner, pairs * pair_rows:, :] = notes[owner * note_rows:(owner + 1) * note_rows, :].astype(jnp.bfloat16)


def grid_kernel(grid_h, w_kv_h, table, grid, w_kv, sems):
    copies = fetch([(grid_h, grid), (w_kv_h, w_kv)], sems)
    width = w_kv.shape[1] // 2
    copies[0].wait()
    normed = norm_rows(grid[...])
    copies[1].wait()
    grid_kv = mm(normed, w_kv[...]).astype(jnp.bfloat16)
    count = grid_kv.shape[0]
    masks = half_masks()
    for pair in range(width // LANES):
        key_pair = grid_kv[:, pair * LANES:(pair + 1) * LANES]
        value_pair = grid_kv[:, width + pair * LANES:width + (pair + 1) * LANES]
        for half in range(2):
            mask = masks[half]
            rows = slice(half * count, (half + 1) * count)
            table[pair, rows, :LANES] = value_pair * mask
            table[pair, rows, LANES:] = jnp.broadcast_to(mask, (count, LANES))
            table[pair, 2 * count:, half * LANES:(half + 1) * LANES] = key_pair * mask


def owner_kernel(block_len, capacity, chunk, recv, table_h, back_h, table, back, bias, sems, outs):
    node_count, message_rows, _ = recv.shape
    pairs, table_rows, _ = table.shape
    key_count = table_rows // 3
    pair_rows = capacity * block_len
    note_rows = message_rows - pairs * pair_rows
    group = chunk // pair_rows
    chunks = node_count // group
    copies = fetch([(table_h.at[pair], table.at[pair]) for pair in range(pairs)], sems)
    tags = recv[:, pairs * pair_rows:, :].reshape(node_count * note_rows, LANES)
    fold = (
        lax.broadcasted_iota(jnp.int32, (block_len, LANES), 1) % block_len
        == lax.broadcasted_iota(jnp.int32, (block_len, LANES), 0)
    ).astype(jnp.float32).astype(jnp.bfloat16)
    columns = mm_nt(fold, tags)
    key_pos = lax.broadcasted_iota(jnp.int32, (block_len, key_count), 1).astype(jnp.float32)

    def make_bias(index):
        for slot in range(index * group * capacity, (index + 1) * group * capacity):
            spot = slot // capacity * note_rows + 2 * (slot % capacity)
            low_part, signed = columns[:, spot:spot + 1], columns[:, spot + 1:spot + 2]
            begin = low_part + jnp.where(signed < 0, 256.0, 0.0)
            end = begin + jnp.maximum(jnp.abs(signed), 1.0)
            inside = (key_pos >= begin) & (key_pos < end)
            bias[slot * block_len:(slot + 1) * block_len, :] = jnp.where(inside, 0.0, NEG)

    low_half = lane_group((chunk, LANES), LANES // 2) == 0
    half_lane = lane_group((HEADS, LANES), LANES // 2)
    log_width = LANES // 2 // pairs
    log_group = lane_group((chunk, LANES), log_width) % pairs
    pick_row = lax.broadcasted_iota(jnp.int32, (HEADS, LANES), 0)
    pick_lane = lax.broadcasted_iota(jnp.int32, (HEADS, LANES), 1)
    pick = (pick_lane == pick_row % 2 * (LANES // 2) + pick_row // 2 * log_width).astype(jnp.float32).astype(jnp.bfloat16)
    steps = [(index, head) for index in range(chunks) for head in range(HEADS)]
    scores, softs, mixes, held_logs = {}, {}, {}, {}
    moves = []
    for turn in range(len(steps) + 4):
        if turn < len(steps):
            index, head = steps[turn]
            pair, half = divmod(head, 2)
            if head == 0:
                make_bias(index)
            if index == 0 and half == 0:
                copies[pair].wait()
            span = slice(index * group, (index + 1) * group)
            rows = recv[span, pair * pair_rows:(pair + 1) * pair_rows, :].reshape(chunk, LANES)
            keys = table[pair, 2 * key_count:, half * LANES:(half + 1) * LANES]
            scores[turn] = mm_nt(rows, keys) + bias[index * chunk:(index + 1) * chunk, :]
        item = scores.pop(turn - 2, None)
        if item is not None:
            top = jnp.max(item, axis=-1, keepdims=True)
            softs[turn - 2] = (top, jnp.exp2(item - top).astype(jnp.bfloat16))
        step = turn - 4
        if step < 0:
            continue
        index, head = steps[step]
        pair, half = divmod(head, 2)
        mixes[step] = mm(softs[step][1], table[pair, half * key_count:(half + 1) * key_count, :])
        if half == 0:
            continue
        mixed = mixes.pop(step - 1) + mixes.pop(step)
        total = mixed[:, LANES:]
        span = slice(index * group, (index + 1) * group)
        part = slice(pair * pair_rows, (pair + 1) * pair_rows)
        back[span, part, :] = (mixed[:, :LANES] / total).astype(jnp.bfloat16).reshape(group, pair_rows, LANES)
        logs = jnp.where(low_half, softs.pop(step - 1)[0], softs.pop(step)[0]) + jnp.log2(total)
        held_logs[index] = jnp.where(log_group == pair, logs, held_logs[index]) if pair else logs
        if pair < pairs - 1:
            continue
        logs = held_logs.pop(index)
        high = logs.astype(jnp.bfloat16)
        log_high = mm_nt(pick, high)
        log_low = mm_nt(pick, (logs - high.astype(jnp.float32)).astype(jnp.bfloat16))
        for offset in range(group):
            lane = offset * pair_rows
            tile, shift = lane // LANES, lane % LANES
            high = log_high[:, tile * LANES:(tile + 1) * LANES]
            low = log_low[:, tile * LANES:(tile + 1) * LANES]
            if shift:
                high = pltpu.roll(high, LANES - shift, 1)
            low_shift = (LANES // 2 - shift) % LANES
            if low_shift:
                low = pltpu.roll(low, low_shift, 1)
            back[index * group + offset, pairs * pair_rows:pairs * pair_rows + HEADS, :] = jnp.where(
                half_lane == 0, high, low
            ).astype(jnp.bfloat16)
        place = pl.ds(index * group, group)
        moves.append(pltpu.make_async_copy(back.at[place], back_h.at[place], outs.at[index]))
        moves[-1].start()
    for item in moves:
        item.wait()


def combine_kernel(block_len, capacity, routes_h, ranks_h, back, attended, routes, ranks, logs, sems):
    node_count, _, _ = back.shape
    width = attended.shape[1]
    pairs = width // LANES
    pair_rows = capacity * block_len
    copies = fetch([(routes_h, routes), (ranks_h, ranks)], sems)
    route_count, block_count = routes.shape
    halves = back[:, pairs * pair_rows:pairs * pair_rows + HEADS, :].astype(jnp.float32).reshape(node_count * HEADS, LANES)
    logs[...] = halves + pltpu.roll(halves, LANES // 2, 1)
    for item in copies:
        item.wait()
    group = lane_group((HEADS, LANES), block_len)
    per_tile = LANES // block_len
    tiles = block_count // per_tile
    route_logs = []
    for route in range(route_count):
        parts = []
        for tile in range(tiles):
            gathered = jnp.zeros((HEADS, LANES), jnp.float32)
            for spot in range(per_tile):
                block = tile * per_tile + spot
                start = pl.multiple_of(routes[route, block] * HEADS, HEADS)
                shift = (spot + per_tile - ranks[route, block]) * block_len % LANES
                moved = pltpu.roll(logs[pl.ds(start, HEADS), :], shift, 1)
                gathered = jnp.where(group == spot, moved, gathered)
            parts.append(gathered)
        route_logs.append(jnp.concatenate(parts, axis=1))
    best = functools.reduce(jnp.maximum, route_logs)
    terms = [jnp.exp2(item - best) for item in route_logs]
    total = functools.reduce(jnp.add, terms)
    spread = (
        lax.broadcasted_iota(jnp.int32, (2 * HEADS, width), 1) // (width // HEADS)
        == lax.broadcasted_iota(jnp.int32, (2 * HEADS, width), 0) % HEADS
    ).astype(jnp.float32).astype(jnp.bfloat16)
    weights = []
    for item in terms:
        share = item / total
        high = share.astype(jnp.bfloat16).astype(jnp.float32)
        both = jnp.concatenate([high, share - high], axis=0).astype(jnp.bfloat16)
        weights.append(mm_tn(both, spread))
    for block in range(block_count):
        rows = slice(block * block_len, (block + 1) * block_len)
        for pair in range(pairs):
            lanes = slice(pair * LANES, (pair + 1) * LANES)
            acc = None
            for route in range(route_count):
                start = pl.multiple_of(pair * pair_rows + ranks[route, block] * block_len, block_len)
                piece = back[routes[route, block], pl.ds(start, block_len), :].astype(jnp.float32)
                piece = piece * weights[route][rows, lanes]
                acc = piece if acc is None else acc + piece
            attended[rows, lanes] = acc.astype(jnp.bfloat16)


def own_kernel(query_scale, mesh_h, attended, w_out_h, w_qkv_h, encoded, own, keyval, mixes,
               mesh, w_out, w_qkv, sems):
    copies = fetch([(w_out_h, w_out), (mesh_h, mesh), (w_qkv_h, w_qkv)], sems)
    width = attended.shape[1]
    for item in copies[:2]:
        item.wait()
    rows = (mesh[...].astype(jnp.float32) + mm(attended[...], w_out[...])).astype(jnp.bfloat16)
    encoded[...] = rows
    own[:, width:] = rows
    normed = norm_rows(rows)
    copies[2].wait()
    query = (mm(normed, w_qkv[:, :width]) * query_scale).astype(jnp.bfloat16)
    own[:, :width] = query
    keyval[...] = mm(normed, w_qkv[:, width:]).astype(jnp.bfloat16)
    low_half = lane_group((rows.shape[0], LANES), LANES // 2) == 0
    masks = half_masks()
    scores, softs, mixed = {}, {}, {}
    for turn in range(HEADS + 2):
        if turn < HEADS:
            lanes = slice(turn // 2 * LANES, (turn // 2 + 1) * LANES)
            scores[turn] = mm_nt(query[:, lanes], keyval[:, lanes] * masks[turn % 2])
        head = turn - 1
        if 0 <= head < HEADS:
            item = scores.pop(head)
            top = jnp.max(item, axis=-1, keepdims=True)
            softs[head] = (top, jnp.exp2(item - top).astype(jnp.bfloat16))
        head = turn - 2
        if head < 0:
            continue
        pair, half = divmod(head, 2)
        value = keyval[:, width + pair * LANES:width + (pair + 1) * LANES]
        table = jnp.concatenate([value * masks[half], jnp.broadcast_to(masks[half], value.shape)], axis=1)
        mixed[half] = mm(softs[head][1], table)
        if half:
            total = mixed[0] + mixed[1]
            mixes[pair, :, :LANES] = total[:, :LANES] / total[:, LANES:]
            top = jnp.where(low_half, softs.pop(head - 1)[0], softs.pop(head)[0])
            mixes[pair, :, LANES:] = top + jnp.log2(total[:, LANES:])


def window_kernel(edges, own, mixes, mesh_far, att_far, chip_kv_h, w_out_h, w_qkv_h, w_proc_h, processed,
                  chip_kv, w_out, w_near, w_proc, mixed, sems):
    rows, width = mixed.shape
    copies = fetch(
        [
            (w_out_h, w_out),
            (w_qkv_h.at[:, pl.ds(width, 2 * width)], w_near),
            (chip_kv_h, chip_kv),
            (w_proc_h, w_proc),
        ],
        sems,
    )
    copies[0].wait()
    far = (mesh_far[...].astype(jnp.float32) + mm(att_far[...], w_out[...])).astype(jnp.bfloat16)
    normed = norm_rows(far)
    copies[1].wait()
    far_kv = mm(normed, w_near[...]).astype(jnp.bfloat16)
    copies[2].wait()
    behind = lax.broadcasted_iota(jnp.int32, (rows, rows), 1) >= lax.broadcasted_iota(jnp.int32, (rows, rows), 0)
    in_far = behind.astype(jnp.int32) != edges[0]
    bias = jnp.where(in_far & (edges[1] == 0), NEG, 0.0)
    low_half = lane_group((rows, LANES), LANES // 2) == 0
    masks = half_masks()
    scores, softs, sums = {}, {}, {}
    for turn in range(HEADS + 2):
        if turn < HEADS:
            lanes = slice(turn // 2 * LANES, (turn // 2 + 1) * LANES)
            mask = masks[turn % 2]
            far_scores = mm_nt(own[:, lanes], far_kv[:, lanes] * mask)
            chip_scores = mm_nt(own[:, lanes], chip_kv[:, lanes] * mask)
            scores[turn] = jnp.where(in_far, far_scores, chip_scores) + bias
        head = turn - 1
        if 0 <= head < HEADS:
            item = scores.pop(head)
            top = jnp.max(item, axis=-1, keepdims=True)
            term = jnp.exp2(item - top)
            first = jnp.where(in_far, term, 0.0)
            softs[head] = (top, jnp.concatenate([first, term - first], axis=1).astype(jnp.bfloat16))
        head = turn - 2
        if head < 0:
            continue
        pair, half = divmod(head, 2)
        lanes = slice(width + pair * LANES, width + (pair + 1) * LANES)
        value = jnp.concatenate([far_kv[:, lanes], chip_kv[:, lanes]], axis=0)
        table = jnp.concatenate([value * masks[half], jnp.broadcast_to(masks[half], value.shape)], axis=1)
        sums[half] = mm(softs[head][1], table)
        if half:
            top = jnp.where(low_half, softs.pop(head - 1)[0], softs.pop(head)[0])
            own_log = mixes[pair, :, LANES:]
            best = jnp.maximum(top, own_log)
            near_part, own_part = jnp.exp2(top - best), jnp.exp2(own_log - best)
            total = sums[0] + sums[1]
            share = total[:, :LANES] * near_part + mixes[pair, :, :LANES] * own_part
            count = total[:, LANES:] * near_part + own_part
            mixed[:, pair * LANES:(pair + 1) * LANES] = (share / count).astype(jnp.bfloat16)
    copies[3].wait()
    processed[...] = (own[:, width:].astype(jnp.float32) + mm(mixed[...], w_proc[...])).astype(jnp.bfloat16)


def call(kernel, outs, out_specs, operands, scratch, cost, limit=LIMIT, near=()):
    return pl.pallas_call(
        kernel,
        out_shape=outs,
        in_specs=[SMEM if item.shape == (2,) else VMEM if i in near else ANY for i, item in enumerate(operands)],
        out_specs=out_specs,
        scratch_shapes=scratch,
        cost_estimate=pl.CostEstimate(flops=cost[0], bytes_accessed=cost[1], transcendentals=cost[2]),
        compiler_params=pltpu.CompilerParams(vmem_limit_bytes=limit),
    )(*operands)


def shape(dims, dtype=jnp.bfloat16):
    return jax.ShapeDtypeStruct(dims, dtype)


def held(item):
    return pltpu.VMEM(item.shape, item.dtype)


def dma(count):
    return pltpu.SemaphoreType.DMA((count,))


def local(grid_feats, mesh_feats, routes, edge_first, edge_count, w_query, w_kv, w_out_enc, w_qkv, w_out_proc):
    width = w_query.shape[1]
    model = mesh_feats.shape[1]
    query_scale = math.log2(math.e) / math.sqrt(width // HEADS)
    node_count = lax.axis_size("outer") * lax.axis_size("inner")
    block_count, route_count = routes.shape
    rows = mesh_feats.shape[0]
    key_count = grid_feats.shape[0]
    block_len = rows // block_count
    capacity = max(1, (block_count * route_count + node_count - 1) // node_count)
    pairs = width // LANES
    pair_rows = capacity * block_len
    note_rows = max(8, -(-2 * capacity // 8) * 8)
    message = shape((node_count, pairs * pair_rows + note_rows, LANES))
    message_bytes = 2 * math.prod(message.shape)
    routes_t, first_t, count_t = routes.T, edge_first.T, edge_count.T
    ranks_shape = shape(routes_t.shape, jnp.int32)
    in_smem = pltpu.SMEM(routes_t.shape, jnp.int32)
    place = (block_len, capacity)

    send, ranks = call(
        functools.partial(send_kernel, *place, query_scale),
        [message, ranks_shape],
        [VMEM, SMEM],
        (routes_t, first_t, count_t, mesh_feats, w_query),
        [in_smem, held(first_t), held(count_t), held(mesh_feats), held(w_query), pltpu.SMEM((node_count,), jnp.int32),
         pltpu.VMEM((node_count * note_rows, LANES), jnp.float32), dma(5)],
        (2 * rows * model * width, 2 * model * (rows + width) + message_bytes, 0),
        None,
    )
    recv = lax.all_to_all(send, AXES, split_axis=0, concat_axis=0, tiled=True)

    table = call(
        grid_kernel,
        shape((pairs, 3 * key_count, 2 * LANES)),
        VMEM,
        (grid_feats, w_kv),
        [held(grid_feats), held(w_kv), dma(2)],
        (4 * key_count * model * width, 2 * model * (key_count + 2 * width) + 12 * key_count * width, 0),
        None,
    )

    on_chip = [(i, i ^ 1) for i in range(node_count)]
    off_chip = [(i, i + 1) for i in range(1, node_count - 1, 2)] + [(i + 1, i) for i in range(1, node_count - 1, 2)]
    late_mesh, table = lax.optimization_barrier((mesh_feats, table))
    mesh_far = lax.ppermute(late_mesh, AXES, off_chip)

    chunk = math.gcd(node_count * pair_rows, 512)
    back = call(
        functools.partial(owner_kernel, *place, chunk),
        message,
        HBM,
        (recv, table),
        [held(table), held(message), pltpu.VMEM((node_count * pair_rows, key_count), jnp.float32), dma(pairs),
         dma(node_count * pair_rows // chunk)],
        (4 * node_count * pair_rows * key_count * width, 2 * message_bytes, node_count * pair_rows * key_count * HEADS),
        near=(0,),
    )
    back = lax.all_to_all(back, AXES, split_axis=0, concat_axis=0, tiled=True)

    attended = call(
        functools.partial(combine_kernel, *place),
        shape((rows, width)),
        VMEM,
        (routes_t, ranks, back),
        [in_smem, in_smem, pltpu.VMEM((node_count * HEADS, LANES), jnp.float32), dma(2)],
        (4 * rows * width * route_count, message_bytes, 0),
        near=(2,),
    )
    att_far = lax.ppermute(attended, AXES, off_chip)

    encoded, own, keyval, mixes = call(
        functools.partial(own_kernel, query_scale),
        [shape((rows, model)), shape((rows, width + model)), shape((rows, 2 * width)),
         shape((pairs, rows, 2 * LANES), jnp.float32)],
        [VMEM] * 4,
        (mesh_feats, attended, w_out_enc, w_qkv),
        [held(mesh_feats), held(w_out_enc), held(w_qkv), dma(3)],
        (8 * rows * model * width, 2 * model * (2 * rows + 4 * width), 0),
        near=(1,),
    )

    chip_kv = lax.ppermute(keyval, AXES, on_chip)
    place_index = lax.axis_index(AXES)
    odd = place_index % 2
    edges = jnp.stack([odd, (place_index + 2 * odd - 1) % (node_count + 1) < node_count]).astype(jnp.int32)
    processed = call(
        window_kernel,
        shape((rows, model)),
        VMEM,
        (edges, own, mixes, mesh_far, att_far, chip_kv, w_out_enc, w_qkv, w_out_proc),
        [held(chip_kv), held(w_out_enc), pltpu.VMEM((model, 2 * width), jnp.bfloat16), held(w_out_proc),
         pltpu.VMEM((rows, width), jnp.bfloat16), dma(4)],
        (16 * rows * model * width, 2 * model * (4 * rows + 5 * width), 3 * rows * rows * HEADS),
        near=range(1, 5),
    )
    return (encoded, processed)


def solution(mesh):
    rows = P(("groups", "outer", "inner"), None)
    return jax.shard_map(
        local,
        mesh=mesh,
        in_specs=(rows,) * 5 + (P(),) * 5,
        out_specs=(rows, rows),
        check_vma=False,
    )
```

profile of v0, /device:TPU:17, one launch (start us, length us, event | category | flops | bytes accessed | tf_op | source)
XLA Modules:
  0.0 99.7 jit_solution(11531136835483140705)
XLA Ops:
  0.6 3.4 %shard_map.113 = (bf16[16,264,128]{2,1,0:T(8,128)(2,1)}, s32[4,16]{1,0:T(4,128)}) custom-call(s32[4,16]{1,0:T(4,128)} %bitcast.5, s32[4,256]{1,0:T(4,128)} %bitcast.7, s32[4,256]{1,0:T(4,128)} %bitcast.8, bf16[256,1024]{1,0:T(8,128)(2,1)} %mesh_h.3, bf16[1024,512]{1,0:T(8,128)(2,1)} %w_query_h.1), custom_call_target="tpu_custom_call" | custom-call | flops 268435456 | bytes 2654208 | tf_op jit(solution)/shard_map/pallas_call | solution.py:375
  4.0 6.5 %all-to-all-start = ((bf16[16,264,128]{2,1,0:T(8,128)(2,1)}), bf16[16,264,128]{2,1,0:T(8,128)(2,1)S(1)}, u32[]{:S(2)}, u32[]{:S(2)}) async-start(bf16[16,264,128]{2,1,0:T(8,128)(2,1)} %get-tuple-element.11), calls=%async_computation | async-start | bytes 2162688 | tf_op jit(solution)/shard_map/all_to_all | solution.py:428
  10.5 4.9 %shard_map.114.table_h = bf16[4,1536,256]{2,1,0:T(8,128)(2,1)} custom-call(bf16[512,1024]{1,0:T(8,128)(2,1)} %grid_h.1, bf16[1024,1024]{1,0:T(8,128)(2,1)} %w_kv_h.1), custom_call_target="tpu_custom_call" | custom-call | flops 1073741824 | bytes 6291456 | tf_op jit(solution)/shard_map/pallas_call | solution.py:375
  15.5 20.3 %all-to-all-done.recv = bf16[16,264,128]{2,1,0:T(8,128)(2,1)S(1)} async-done(((bf16[16,264,128]{2,1,0:T(8,128)(2,1)}), bf16[16,264,128]{2,1,0:T(8,128)(2,1)S(1)}, u32[]{:S(2)}, u32[]{:S(2)}) %all-to-all-start) | async-done | bytes 1081376 | tf_op jit(solution)/shard_map/all_to_all | solution.py:428
  35.8 9.4 %shard_map.115 = bf16[16,264,128]{2,1,0:T(8,128)(2,1)} custom-call(bf16[16,264,128]{2,1,0:T(8,128)(2,1)S(1)} %all-to-all-done.recv, bf16[4,1536,256]{2,1,0:T(8,128)(2,1)} %shard_map.114.table_h), custom_call_target="tpu_custom_call" | custom-call | flops 1073741824 | bytes 2162688 | tf_op jit(solution)/shard_map/pallas_call | solution.py:375
  45.2 0.0 copy-start
  45.2 0.0 copy-start.1
  45.2 0.0 copy-start.2
  45.2 5.3 %all-to-all-start.1 = ((bf16[16,264,128]{2,1,0:T(8,128)(2,1)}), bf16[16,264,128]{2,1,0:T(8,128)(2,1)S(1)}, u32[]{:S(2)}, u32[]{:S(2)}) async-start(bf16[16,264,128]{2,1,0:T(8,128)(2,1)} %shard_map.115), calls=%async_computation.1 | async-start | bytes 2162688 | tf_op jit(solution)/shard_map/all_to_all | solution.py:456
  50.5 0.0 copy-done
  50.5 3.6 %collective-permute-start = (bf16[256,1024]{1,0:T(8,128)(2,1)S(1)}, bf16[256,1024]{1,0:T(8,128)(2,1)S(1)}, u32[]{:S(2)}, u32[]{:S(2)}) collective-permute-start(bf16[256,1024]{1,0:T(8,128)(2,1)S(1)} %copy-done), channel_id=1, source_target_pairs={{1,2},{3,4},{5,6},{7,8},{9,10},{11,12},{13,14},{2,1},{4,3},{6,5},{... | collective-permute-start | bytes 1572872 | tf_op jit(solution)/shard_map/ppermute | solution.py:443
  54.1 21.8 %all-to-all-done.1.back = bf16[16,264,128]{2,1,0:T(8,128)(2,1)S(1)} async-done(((bf16[16,264,128]{2,1,0:T(8,128)(2,1)}), bf16[16,264,128]{2,1,0:T(8,128)(2,1)S(1)}, u32[]{:S(2)}, u32[]{:S(2)}) %all-to-all-start.1) | async-done | bytes 1081376 | tf_op jit(solution)/shard_map/all_to_all | solution.py:456
  75.8 0.0 copy-done.1
  75.8 0.0 copy-done.2
  75.9 1.5 %shard_map.116.attended = bf16[256,512]{1,0:T(8,128)(2,1)S(1)} custom-call(s32[4,16]{1,0:T(4,128)S(1)} %bitcast.6, s32[4,16]{1,0:T(4,128)S(1)} %copy-done.2, bf16[16,264,128]{2,1,0:T(8,128)(2,1)S(1)} %all-to-all-done.1.back), custom_call_target="tpu_custom_call" | custom-call | flops 2097152 | bytes 1081344 | tf_op jit(solution)/shard_map/pallas_call | solution.py:375
  77.4 4.1 %shard_map.117 = (bf16[256,1024]{1,0:T(8,128)(2,1)}, bf16[256,1536]{1,0:T(8,128)(2,1)S(1)}, bf16[256,1024]{1,0:T(8,128)(2,1)}, f32[4,256,256]{2,1,0:T(8,128)S(1)}) custom-call(bf16[256,1024]{1,0:T(8,128)(2,1)S(1)} %copy-done, bf16[256,512]{1,0:T(8,128)(2,1)S(1)} %shard_map.116.attended, bf16[512,1024]{1,0:T(8,128)(2,1)} %w_out_h.3, bf16[1024,1536]{1,0:T(8,128)(2,1)} %w_qkv_h.3), custom_call_target="tpu_custom_call" | custom-call | flops 1073741824 | bytes 5242880 | tf_op jit(solution)/shard_map/pallas_call | solution.py:375
  81.5 1.6 %collective-permute-start.2 = (bf16[256,1024]{1,0:T(8,128)(2,1)}, bf16[256,1024]{1,0:T(8,128)(2,1)}, u32[]{:S(2)}, u32[]{:S(2)}) collective-permute-start(bf16[256,1024]{1,0:T(8,128)(2,1)} %get-tuple-element.17), channel_id=1, source_target_pairs={{0,1},{1,0},{2,3},{3,2},{4,5},{5,4},{6,7},{7,6},{8,9},{9,8},{10,11... | collective-permute-start | bytes 1572872 | tf_op jit(solution)/shard_map/ppermute | solution.py:480
  83.1 1.9 %collective-permute-start.1 = (bf16[256,512]{1,0:T(8,128)(2,1)S(1)}, bf16[256,512]{1,0:T(8,128)(2,1)S(1)}, u32[]{:S(2)}, u32[]{:S(2)}) collective-permute-start(bf16[256,512]{1,0:T(8,128)(2,1)S(1)} %shard_map.116.attended), channel_id=1, source_target_pairs={{1,2},{3,4},{5,6},{7,8},{9,10},{11,12},{13,14},{2,1},{4,3},{6,5},{... | collective-permute-start | bytes 786440 | tf_op jit(solution)/shard_map/ppermute | solution.py:467
  85.0 0.1 pad_add_fusion.edges
  85.1 0.0 collective-permute-done.mesh_far
  85.1 8.5 %collective-permute-done.1.att_far = bf16[256,512]{1,0:T(8,128)(2,1)S(1)} collective-permute-done((bf16[256,512]{1,0:T(8,128)(2,1)S(1)}, bf16[256,512]{1,0:T(8,128)(2,1)S(1)}, u32[]{:S(2)}, u32[]{:S(2)}) %collective-permute-start.1) | collective-permute-done | bytes 262176 | tf_op jit(solution)/shard_map/ppermute | solution.py:467
  93.6 0.0 collective-permute-done.2.chip_kv_h
  93.6 6.0 %shard_map.118 = bf16[256,1024]{1,0:T(8,128)(2,1)} custom-call(s32[2]{0:T(128)S(1)} %pad_add_fusion.edges, bf16[256,1536]{1,0:T(8,128)(2,1)S(1)} %get-tuple-element.14.own, f32[4,256,256]{2,1,0:T(8,128)S(1)} %get-tuple-element.15.mixes, bf16[256,1024]{1,0:T(8,128)(2,1)S(1)} %collective-permute-done.mesh_far, ...), custom_call_target="tpu_custom_call" | custom-call | flops 2147483648 | bytes 7340032 | tf_op jit(solution)/shard_map/pallas_call | solution.py:375
Async XLA Ops:
  4.0 31.7 %all-to-all-start = ((bf16[16,264,128]{2,1,0:T(8,128)(2,1)}), bf16[16,264,128]{2,1,0:T(8,128)(2,1)S(1)}, u32[]{:S(2)}, u32[]{:S(2)}) async-start(bf16[16,264,128]{2,1,0:T(8,128)(2,1)} %get-tuple-element.11), calls=%async_computation | async-start | bytes 2162688 | tf_op jit(solution)/shard_map/all_to_all | solution.py:428
  45.2 5.3 %copy-start = (bf16[256,1024]{1,0:T(8,128)(2,1)S(1)}, bf16[256,1024]{1,0:T(8,128)(2,1)}, u32[]{:S(2)}) copy-start(bf16[256,1024]{1,0:T(8,128)(2,1)} %mesh_h.3) | copy-start | bytes 1572868
  45.2 30.7 %copy-start.1 = (s32[16,4]{0,1:T(4,128)S(1)}, s32[16,4]{0,1:T(4,128)}, u32[]{:S(2)}) copy-start(s32[16,4]{0,1:T(4,128)} %param.12) | copy-start | bytes 772
  45.2 30.6 %copy-start.2 = (s32[4,16]{1,0:T(4,128)S(1)}, s32[4,16]{1,0:T(4,128)}, u32[]{:S(2)}) copy-start(s32[4,16]{1,0:T(4,128)} %get-tuple-element.10.ranks_h) | copy-start | bytes 772
  45.2 30.6 %all-to-all-start.1 = ((bf16[16,264,128]{2,1,0:T(8,128)(2,1)}), bf16[16,264,128]{2,1,0:T(8,128)(2,1)S(1)}, u32[]{:S(2)}, u32[]{:S(2)}) async-start(bf16[16,264,128]{2,1,0:T(8,128)(2,1)} %shard_map.115), calls=%async_computation.1 | async-start | bytes 2162688 | tf_op jit(solution)/shard_map/all_to_all | solution.py:456
  50.5 34.6 %collective-permute-start = (bf16[256,1024]{1,0:T(8,128)(2,1)S(1)}, bf16[256,1024]{1,0:T(8,128)(2,1)S(1)}, u32[]{:S(2)}, u32[]{:S(2)}) collective-permute-start(bf16[256,1024]{1,0:T(8,128)(2,1)S(1)} %copy-done), channel_id=1, source_target_pairs={{1,2},{3,4},{5,6},{7,8},{9,10},{11,12},{13,14},{2,1},{4,3},{6,5},{... | collective-permute-start | bytes 1572872 | tf_op jit(solution)/shard_map/ppermute | solution.py:443
  81.5 12.1 %collective-permute-start.2 = (bf16[256,1024]{1,0:T(8,128)(2,1)}, bf16[256,1024]{1,0:T(8,128)(2,1)}, u32[]{:S(2)}, u32[]{:S(2)}) collective-permute-start(bf16[256,1024]{1,0:T(8,128)(2,1)} %get-tuple-element.17), channel_id=1, source_target_pairs={{0,1},{1,0},{2,3},{3,2},{4,5},{5,4},{6,7},{7,6},{8,9},{9,8},{10,11... | collective-permute-start | bytes 1572872 | tf_op jit(solution)/shard_map/ppermute | solution.py:480
  83.1 10.5 %collective-permute-start.1 = (bf16[256,512]{1,0:T(8,128)(2,1)S(1)}, bf16[256,512]{1,0:T(8,128)(2,1)S(1)}, u32[]{:S(2)}, u32[]{:S(2)}) collective-permute-start(bf16[256,512]{1,0:T(8,128)(2,1)S(1)} %shard_map.116.attended), channel_id=1, source_target_pairs={{1,2},{3,4},{5,6},{7,8},{9,10},{11,12},{13,14},{2,1},{4,3},{6,5},{... | collective-permute-start | bytes 786440 | tf_op jit(solution)/shard_map/ppermute | solution.py:467
where the time goes:
time: 100 us; the launch traced here: 99.7 us
  waiting for transfers between devices  50.6 us (51%)
  Pallas kernels  29.3 us (29%)
  starting transfers between devices  18.8 us (19%)
    pallas_call x6, Pallas kernels, call(): pl.pallas_call(kernel, out_shape=outs, in_specs=[SMEM if item.shape == (2...  29.3 us
    all_to_all x1, waiting for transfers between devices, local(): back = lax.all_to_all(back, AXES, split_axis=0, concat_axis=0, tiled=True)  21.8 us
    all_to_all x1, waiting for transfers between devices, local(): recv = lax.all_to_all(send, AXES, split_axis=0, concat_axis=0, tiled=True)  20.3 us
    ppermute x1, waiting for transfers between devices, local(): att_far = lax.ppermute(attended, AXES, off_chip)  8.46 us
    all_to_all x1, starting transfers between devices, local(): recv = lax.all_to_all(send, AXES, split_axis=0, concat_axis=0, tiled=True)  6.48 us
    all_to_all x1, starting transfers between devices, local(): back = lax.all_to_all(back, AXES, split_axis=0, concat_axis=0, tiled=True)  5.27 us
    ppermute x1, starting transfers between devices, local(): mesh_far = lax.ppermute(late_mesh, AXES, off_chip)  3.55 us
  transfers between devices with their start and end apart: 5, of which 3 were waited for; matrix products, arithmetic and copies ran while one was open for 0% of the time, Pallas kernels for 11%

commit v1 on v0

--- a/solution.py
+++ b/solution.py
@@ -152,6 +152,8 @@
             inside = (key_pos >= begin) & (key_pos < end)
             bias[slot * block_len:(slot + 1) * block_len, :] = jnp.where(inside, 0.0, NEG)
 
+    for index in range(chunks):
+        make_bias(index)
     low_half = lane_group((chunk, LANES), LANES // 2) == 0
     half_lane = lane_group((HEADS, LANES), LANES // 2)
     log_width = LANES // 2 // pairs
@@ -166,8 +168,6 @@
         if turn < len(steps):
             index, head = steps[turn]
             pair, half = divmod(head, 2)
-            if head == 0:
-                make_bias(index)
             if index == 0 and half == 0:
                 copies[pair].wait()
             span = slice(index * group, (index + 1) * group)
@@ -193,6 +193,11 @@
         back[span, part, :] = (mixed[:, :LANES] / total).astype(jnp.bfloat16).reshape(group, pair_rows, LANES)
         logs = jnp.where(low_half, softs.pop(step - 1)[0], softs.pop(step)[0]) + jnp.log2(total)
         held_logs[index] = jnp.where(log_group == pair, logs, held_logs[index]) if pair else logs
+        last = index == chunks - 1
+        if last and pair < pairs - 1:
+            place = (pl.ds(index * group, group), pl.ds(pair * pair_rows, pair_rows))
+            moves.append(pltpu.make_async_copy(back.at[place], back_h.at[place], outs.at[chunks + pair]))
+            moves[-1].start()
         if pair < pairs - 1:
             continue
         logs = held_logs.pop(index)
@@ -212,7 +217,8 @@
             back[index * group + offset, pairs * pair_rows:pairs * pair_rows + HEADS, :] = jnp.where(
                 half_lane == 0, high, low
             ).astype(jnp.bfloat16)
-        place = pl.ds(index * group, group)
+        first_row = (pairs - 1) * pair_rows if last else 0
+        place = (pl.ds(index * group, group), pl.ds(first_row, message_rows - first_row))
         moves.append(pltpu.make_async_copy(back.at[place], back_h.at[place], outs.at[index]))
         moves[-1].start()
     for item in moves:
@@ -274,8 +280,17 @@
 
 def own_kernel(query_scale, mesh_h, attended, w_out_h, w_qkv_h, encoded, own, keyval, mixes,
                mesh, w_out, w_qkv, sems):
-    copies = fetch([(w_out_h, w_out), (mesh_h, mesh), (w_qkv_h, w_qkv)], sems)
     width = attended.shape[1]
+    query_part, other_part = pl.ds(0, width), pl.ds(width, 2 * width)
+    copies = fetch(
+        [
+            (w_out_h, w_out),
+            (mesh_h, mesh),
+            (w_qkv_h.at[:, query_part], w_qkv.at[:, query_part]),
+            (w_qkv_h.at[:, other_part], w_qkv.at[:, other_part]),
+        ],
+        sems,
+    )
     for item in copies[:2]:
         item.wait()
     rows = (mesh[...].astype(jnp.float32) + mm(attended[...], w_out[...])).astype(jnp.bfloat16)
@@ -285,6 +300,7 @@
     copies[2].wait()
     query = (mm(normed, w_qkv[:, :width]) * query_scale).astype(jnp.bfloat16)
     own[:, :width] = query
+    copies[3].wait()
     keyval[...] = mm(normed, w_qkv[:, width:]).astype(jnp.bfloat16)
     low_half = lane_group((rows.shape[0], LANES), LANES // 2) == 0
     masks = half_masks()
@@ -313,23 +329,27 @@
 
 
 def window_kernel(edges, own, mixes, mesh_far, att_far, chip_kv_h, w_out_h, w_qkv_h, w_proc_h, processed,
-                  chip_kv, w_out, w_near, w_proc, mixed, sems):
+                  chip_kv, w_out, w_near, w_proc, mixed, chip_all, sems):
     rows, width = mixed.shape
     copies = fetch(
         [
+            (chip_kv_h, chip_kv),
             (w_out_h, w_out),
             (w_qkv_h.at[:, pl.ds(width, 2 * width)], w_near),
-            (chip_kv_h, chip_kv),
             (w_proc_h, w_proc),
         ],
         sems,
     )
+    masks = half_masks()
     copies[0].wait()
+    for head in range(HEADS):
+        lanes = slice(head // 2 * LANES, (head // 2 + 1) * LANES)
+        chip_all[head] = mm_nt(own[:, lanes], chip_kv[:, lanes] * masks[head % 2])
+    copies[1].wait()
     far = (mesh_far[...].astype(jnp.float32) + mm(att_far[...], w_out[...])).astype(jnp.bfloat16)
     normed = norm_rows(far)
-    copies[1].wait()
+    copies[2].wait()
     far_kv = mm(normed, w_near[...]).astype(jnp.bfloat16)
-    copies[2].wait()
     behind = lax.broadcasted_iota(jnp.int32, (rows, rows), 1) >= lax.broadcasted_iota(jnp.int32, (rows, rows), 0)
     in_far = behind.astype(jnp.int32) != edges[0]
     bias = jnp.where(in_far & (edges[1] == 0), NEG, 0.0)
@@ -339,10 +359,8 @@
     for turn in range(HEADS + 2):
         if turn < HEADS:
             lanes = slice(turn // 2 * LANES, (turn // 2 + 1) * LANES)
-            mask = masks[turn % 2]
-            far_scores = mm_nt(own[:, lanes], far_kv[:, lanes] * mask)
-            chip_scores = mm_nt(own[:, lanes], chip_kv[:, lanes] * mask)
-            scores[turn] = jnp.where(in_far, far_scores, chip_scores) + bias
+            far_scores = mm_nt(own[:, lanes], far_kv[:, lanes] * masks[turn % 2])
+            scores[turn] = jnp.where(in_far, far_scores, chip_all[turn]) + bias
         head = turn - 1
         if 0 <= head < HEADS:
             item = scores.pop(head)
@@ -449,7 +467,7 @@
         HBM,
         (recv, table),
         [held(table), held(message), pltpu.VMEM((node_count * pair_rows, key_count), jnp.float32), dma(pairs),
-         dma(node_count * pair_rows // chunk)],
+         dma(node_count * pair_rows // chunk + pairs)],
         (4 * node_count * pair_rows * key_count * width, 2 * message_bytes, node_count * pair_rows * key_count * HEADS),
         near=(0,),
     )
@@ -472,7 +490,7 @@
          shape((pairs, rows, 2 * LANES), jnp.float32)],
         [VMEM] * 4,
         (mesh_feats, attended, w_out_enc, w_qkv),
-        [held(mesh_feats), held(w_out_enc), held(w_qkv), dma(3)],
+        [held(mesh_feats), held(w_out_enc), held(w_qkv), dma(4)],
         (8 * rows * model * width, 2 * model * (2 * rows + 4 * width), 0),
         near=(1,),
     )
@@ -487,7 +505,7 @@
         VMEM,
         (edges, own, mixes, mesh_far, att_far, chip_kv, w_out_enc, w_qkv, w_out_proc),
         [held(chip_kv), held(w_out_enc), pltpu.VMEM((model, 2 * width), jnp.bfloat16), held(w_out_proc),
-         pltpu.VMEM((rows, width), jnp.bfloat16), dma(4)],
+         pltpu.VMEM((rows, width), jnp.bfloat16), pltpu.VMEM((HEADS, rows, rows), jnp.float32), dma(4)],
         (16 * rows * model * width, 2 * model * (4 * rows + 5 * width), 3 * rows * rows * HEADS),
         near=range(1, 5),
     )

time: 100 us -> 99.8 us (level)
  transfers between devices with their start and end apart: 5 -> 5, of which waited for: 3 -> 3; matrix products, arithmetic and copies ran while one was open for 0% -> 0% of each run, Pallas kernels for 11% -> 10%
where the time goes in v1:
time: 99.8 us; the launch traced here: 99.5 us
  waiting for transfers between devices  50.6 us (51%)
  Pallas kernels  29.1 us (29%)
  starting transfers between devices  18.8 us (19%)
    pallas_call x6, Pallas kernels, call(): pl.pallas_call(kernel, out_shape=outs, in_specs=[SMEM if item.shape == (2...  29.1 us
    all_to_all x1, waiting for transfers between devices, local(): back = lax.all_to_all(back, AXES, split_axis=0, concat_axis=0, tiled=True)  21.8 us
    all_to_all x1, waiting for transfers between devices, local(): recv = lax.all_to_all(send, AXES, split_axis=0, concat_axis=0, tiled=True)  20.3 us
    ppermute x1, waiting for transfers between devices, local(): att_far = lax.ppermute(attended, AXES, off_chip)  8.46 us
    all_to_all x1, starting transfers between devices, local(): recv = lax.all_to_all(send, AXES, split_axis=0, concat_axis=0, tiled=True)  6.48 us
    all_to_all x1, starting transfers between devices, local(): back = lax.all_to_all(back, AXES, split_axis=0, concat_axis=0, tiled=True)  5.26 us
    ppermute x1, starting transfers between devices, local(): mesh_far = lax.ppermute(late_mesh, AXES, off_chip)  3.55 us
  transfers between devices with their start and end apart: 5, of which 3 were waited for; matrix products, arithmetic and copies ran while one was open for 0% of the time, Pallas kernels for 10%

profile of v1, /device:TPU:17, one launch (start us, length us, event | category | flops | bytes accessed | tf_op | source)
XLA Modules:
  0.0 99.5 jit_solution(5672413817960617257)
XLA Ops:
  0.6 3.4 %shard_map.113 = (bf16[16,264,128]{2,1,0:T(8,128)(2,1)}, s32[4,16]{1,0:T(4,128)}) custom-call(s32[4,16]{1,0:T(4,128)} %bitcast.5, s32[4,256]{1,0:T(4,128)} %bitcast.7, s32[4,256]{1,0:T(4,128)} %bitcast.8, bf16[256,1024]{1,0:T(8,128)(2,1)} %mesh_h.3, bf16[1024,512]{1,0:T(8,128)(2,1)} %w_query_h.1), custom_call_target="tpu_custom_call" | custom-call | flops 268435456 | bytes 2654208 | tf_op jit(solution)/shard_map/pallas_call | solution.py:393
  4.0 6.5 %all-to-all-start = ((bf16[16,264,128]{2,1,0:T(8,128)(2,1)}), bf16[16,264,128]{2,1,0:T(8,128)(2,1)S(1)}, u32[]{:S(2)}, u32[]{:S(2)}) async-start(bf16[16,264,128]{2,1,0:T(8,128)(2,1)} %get-tuple-element.11), calls=%async_computation | async-start | bytes 2162688 | tf_op jit(solution)/shard_map/all_to_all | solution.py:446
  10.5 4.9 %shard_map.114.table_h = bf16[4,1536,256]{2,1,0:T(8,128)(2,1)} custom-call(bf16[512,1024]{1,0:T(8,128)(2,1)} %grid_h.1, bf16[1024,1024]{1,0:T(8,128)(2,1)} %w_kv_h.1), custom_call_target="tpu_custom_call" | custom-call | flops 1073741824 | bytes 6291456 | tf_op jit(solution)/shard_map/pallas_call | solution.py:393
  15.5 20.3 %all-to-all-done.recv = bf16[16,264,128]{2,1,0:T(8,128)(2,1)S(1)} async-done(((bf16[16,264,128]{2,1,0:T(8,128)(2,1)}), bf16[16,264,128]{2,1,0:T(8,128)(2,1)S(1)}, u32[]{:S(2)}, u32[]{:S(2)}) %all-to-all-start) | async-done | bytes 1081376 | tf_op jit(solution)/shard_map/all_to_all | solution.py:446
  35.8 9.3 %shard_map.115 = bf16[16,264,128]{2,1,0:T(8,128)(2,1)} custom-call(bf16[16,264,128]{2,1,0:T(8,128)(2,1)S(1)} %all-to-all-done.recv, bf16[4,1536,256]{2,1,0:T(8,128)(2,1)} %shard_map.114.table_h), custom_call_target="tpu_custom_call" | custom-call | flops 1073741824 | bytes 2162688 | tf_op jit(solution)/shard_map/pallas_call | solution.py:393
  45.1 0.0 copy-start
  45.1 0.0 copy-start.1
  45.2 0.0 copy-start.2
  45.2 5.3 %all-to-all-start.1 = ((bf16[16,264,128]{2,1,0:T(8,128)(2,1)}), bf16[16,264,128]{2,1,0:T(8,128)(2,1)S(1)}, u32[]{:S(2)}, u32[]{:S(2)}) async-start(bf16[16,264,128]{2,1,0:T(8,128)(2,1)} %shard_map.115), calls=%async_computation.1 | async-start | bytes 2162688 | tf_op jit(solution)/shard_map/all_to_all | solution.py:474
  50.4 0.0 copy-done
  50.4 3.6 %collective-permute-start = (bf16[256,1024]{1,0:T(8,128)(2,1)S(1)}, bf16[256,1024]{1,0:T(8,128)(2,1)S(1)}, u32[]{:S(2)}, u32[]{:S(2)}) collective-permute-start(bf16[256,1024]{1,0:T(8,128)(2,1)S(1)} %copy-done), channel_id=1, source_target_pairs={{1,2},{3,4},{5,6},{7,8},{9,10},{11,12},{13,14},{2,1},{4,3},{6,5},{... | collective-permute-start | bytes 1572872 | tf_op jit(solution)/shard_map/ppermute | solution.py:461
  54.0 21.8 %all-to-all-done.1.back = bf16[16,264,128]{2,1,0:T(8,128)(2,1)S(1)} async-done(((bf16[16,264,128]{2,1,0:T(8,128)(2,1)}), bf16[16,264,128]{2,1,0:T(8,128)(2,1)S(1)}, u32[]{:S(2)}, u32[]{:S(2)}) %all-to-all-start.1) | async-done | bytes 1081376 | tf_op jit(solution)/shard_map/all_to_all | solution.py:474
  75.8 0.0 copy-done.1
  75.8 0.0 copy-done.2
  75.8 1.5 %shard_map.116.attended = bf16[256,512]{1,0:T(8,128)(2,1)S(1)} custom-call(s32[4,16]{1,0:T(4,128)S(1)} %bitcast.6, s32[4,16]{1,0:T(4,128)S(1)} %copy-done.2, bf16[16,264,128]{2,1,0:T(8,128)(2,1)S(1)} %all-to-all-done.1.back), custom_call_target="tpu_custom_call" | custom-call | flops 2097152 | bytes 1081344 | tf_op jit(solution)/shard_map/pallas_call | solution.py:393
  77.3 4.0 %shard_map.117 = (bf16[256,1024]{1,0:T(8,128)(2,1)}, bf16[256,1536]{1,0:T(8,128)(2,1)S(1)}, bf16[256,1024]{1,0:T(8,128)(2,1)}, f32[4,256,256]{2,1,0:T(8,128)S(1)}) custom-call(bf16[256,1024]{1,0:T(8,128)(2,1)S(1)} %copy-done, bf16[256,512]{1,0:T(8,128)(2,1)S(1)} %shard_map.116.attended, bf16[512,1024]{1,0:T(8,128)(2,1)} %w_out_h.3, bf16[1024,1536]{1,0:T(8,128)(2,1)} %w_qkv_h.3), custom_call_target="tpu_custom_call" | custom-call | flops 1073741824 | bytes 5242880 | tf_op jit(solution)/shard_map/pallas_call | solution.py:393
  81.3 1.6 %collective-permute-start.2 = (bf16[256,1024]{1,0:T(8,128)(2,1)}, bf16[256,1024]{1,0:T(8,128)(2,1)}, u32[]{:S(2)}, u32[]{:S(2)}) collective-permute-start(bf16[256,1024]{1,0:T(8,128)(2,1)} %get-tuple-element.17), channel_id=1, source_target_pairs={{0,1},{1,0},{2,3},{3,2},{4,5},{5,4},{6,7},{7,6},{8,9},{9,8},{10,11... | collective-permute-start | bytes 1572872 | tf_op jit(solution)/shard_map/ppermute | solution.py:498
  82.9 1.9 %collective-permute-start.1 = (bf16[256,512]{1,0:T(8,128)(2,1)S(1)}, bf16[256,512]{1,0:T(8,128)(2,1)S(1)}, u32[]{:S(2)}, u32[]{:S(2)}) collective-permute-start(bf16[256,512]{1,0:T(8,128)(2,1)S(1)} %shard_map.116.attended), channel_id=1, source_target_pairs={{1,2},{3,4},{5,6},{7,8},{9,10},{11,12},{13,14},{2,1},{4,3},{6,5},{... | collective-permute-start | bytes 786440 | tf_op jit(solution)/shard_map/ppermute | solution.py:485
  84.9 0.1 pad_add_fusion.edges
  84.9 0.0 collective-permute-done.mesh_far
  84.9 8.5 %collective-permute-done.1.att_far = bf16[256,512]{1,0:T(8,128)(2,1)S(1)} collective-permute-done((bf16[256,512]{1,0:T(8,128)(2,1)S(1)}, bf16[256,512]{1,0:T(8,128)(2,1)S(1)}, u32[]{:S(2)}, u32[]{:S(2)}) %collective-permute-start.1) | collective-permute-done | bytes 262176 | tf_op jit(solution)/shard_map/ppermute | solution.py:485
  93.4 0.0 collective-permute-done.2.chip_kv_h
  93.4 5.9 %shard_map.118 = bf16[256,1024]{1,0:T(8,128)(2,1)} custom-call(s32[2]{0:T(128)S(1)} %pad_add_fusion.edges, bf16[256,1536]{1,0:T(8,128)(2,1)S(1)} %get-tuple-element.14.own, f32[4,256,256]{2,1,0:T(8,128)S(1)} %get-tuple-element.15.mixes, bf16[256,1024]{1,0:T(8,128)(2,1)S(1)} %collective-permute-done.mesh_far, ...), custom_call_target="tpu_custom_call" | custom-call | flops 2147483648 | bytes 7340032 | tf_op jit(solution)/shard_map/pallas_call | solution.py:393
Async XLA Ops:
  4.0 31.7 %all-to-all-start = ((bf16[16,264,128]{2,1,0:T(8,128)(2,1)}), bf16[16,264,128]{2,1,0:T(8,128)(2,1)S(1)}, u32[]{:S(2)}, u32[]{:S(2)}) async-start(bf16[16,264,128]{2,1,0:T(8,128)(2,1)} %get-tuple-element.11), calls=%async_computation | async-start | bytes 2162688 | tf_op jit(solution)/shard_map/all_to_all | solution.py:446
  45.1 5.3 %copy-start = (bf16[256,1024]{1,0:T(8,128)(2,1)S(1)}, bf16[256,1024]{1,0:T(8,128)(2,1)}, u32[]{:S(2)}) copy-start(bf16[256,1024]{1,0:T(8,128)(2,1)} %mesh_h.3) | copy-start | bytes 1572868
  45.1 30.6 %copy-start.1 = (s32[16,4]{0,1:T(4,128)S(1)}, s32[16,4]{0,1:T(4,128)}, u32[]{:S(2)}) copy-start(s32[16,4]{0,1:T(4,128)} %param.12) | copy-start | bytes 772
  45.2 30.6 %copy-start.2 = (s32[4,16]{1,0:T(4,128)S(1)}, s32[4,16]{1,0:T(4,128)}, u32[]{:S(2)}) copy-start(s32[4,16]{1,0:T(4,128)} %get-tuple-element.10.ranks_h) | copy-start | bytes 772
  45.2 30.6 %all-to-all-start.1 = ((bf16[16,264,128]{2,1,0:T(8,128)(2,1)}), bf16[16,264,128]{2,1,0:T(8,128)(2,1)S(1)}, u32[]{:S(2)}, u32[]{:S(2)}) async-start(bf16[16,264,128]{2,1,0:T(8,128)(2,1)} %shard_map.115), calls=%async_computation.1 | async-start | bytes 2162688 | tf_op jit(solution)/shard_map/all_to_all | solution.py:474
  50.4 34.5 %collective-permute-start = (bf16[256,1024]{1,0:T(8,128)(2,1)S(1)}, bf16[256,1024]{1,0:T(8,128)(2,1)S(1)}, u32[]{:S(2)}, u32[]{:S(2)}) collective-permute-start(bf16[256,1024]{1,0:T(8,128)(2,1)S(1)} %copy-done), channel_id=1, source_target_pairs={{1,2},{3,4},{5,6},{7,8},{9,10},{11,12},{13,14},{2,1},{4,3},{6,5},{... | collective-permute-start | bytes 1572872 | tf_op jit(solution)/shard_map/ppermute | solution.py:461
  81.3 12.1 %collective-permute-start.2 = (bf16[256,1024]{1,0:T(8,128)(2,1)}, bf16[256,1024]{1,0:T(8,128)(2,1)}, u32[]{:S(2)}, u32[]{:S(2)}) collective-permute-start(bf16[256,1024]{1,0:T(8,128)(2,1)} %get-tuple-element.17), channel_id=1, source_target_pairs={{0,1},{1,0},{2,3},{3,2},{4,5},{5,4},{6,7},{7,6},{8,9},{9,8},{10,11... | collective-permute-start | bytes 1572872 | tf_op jit(solution)/shard_map/ppermute | solution.py:498
  82.9 10.5 %collective-permute-start.1 = (bf16[256,512]{1,0:T(8,128)(2,1)S(1)}, bf16[256,512]{1,0:T(8,128)(2,1)S(1)}, u32[]{:S(2)}, u32[]{:S(2)}) collective-permute-start(bf16[256,512]{1,0:T(8,128)(2,1)S(1)} %shard_map.116.attended), channel_id=1, source_target_pairs={{1,2},{3,4},{5,6},{7,8},{9,10},{11,12},{13,14},{2,1},{4,3},{6,5},{... | collective-permute-start | bytes 786440 | tf_op jit(solution)/shard_map/ppermute | solution.py:485
